TPU v7x, 128 devices: a whole 4x4x4 slice. The times are simulated.
128 devices in a mesh: gx: 8 (over z, core), gy: 4 (over x), gz: 4 (over y).
Axes of the slice: x: 4, y: 4, z: 4, core: 2. Of those that a mesh axis runs over, the one named last changes fastest.
Arguments:
- source_residual: float32 [64, 256, 1024], P('gz', 'gx', 'gy'), may hold values from -8 to 8
- storage: float32 [64, 256, 1024], P('gz', 'gx', 'gy'), may hold values from 0.05 to 3
- conductivity: float32 [64, 256, 1024], P('gz', 'gx', 'gy'), may hold values from 0.05 to 2
- primal_label: int32 [64, 256, 4], P('gz', 'gx', 'gy'), may hold values from 0 to 31
- zone_of_block: int32 [16384, 1], P(('gx', 'gy', 'gz')), may hold values from 0 to 127; in each aligned block of 128 rows (0 to 127, 128 to 255, ...) at most 4 rows name the same one
- coarse_factor: float32 [4096, 4096], P(('gx', 'gy', 'gz')), may hold values from -0.0009765625 to 0.0009765625
- zone_factor: bfloat16 [128, 256, 256], P(('gx', 'gy', 'gz')), may hold values from -0.375 to 0.375
Outputs:
- solution: float32 [64, 256, 1024], P('gz', 'gx', 'gy')
- residual: float32 [64, 256, 1024], P('gz', 'gx', 'gy')
Inputs may be any that keep to these rules, and one draw needn't show every extreme that they name: `zone_of_block`: among the face blocks of one subdomain, no zone is named more than 4 times.
All inputs are finite; a program needn't handle non-finite values.
Results may differ from a plain program's by a relative error of at most 0.018.
Values may be sent and summed in bfloat16 or wider, within the bound.
No kernel may reach another device: no remote copies, remote signals or barrier semaphores. Data moves between devices by JAX's collectives and lax.ppermute only.
A program may use at most 64 MiB of HBM per device.

v0:
```python
import jax
import jax.numpy as jnp
from jax import lax
from jax.sharding import PartitionSpec as P

FB = 256
KC = 32
INNER = 8
ITERS = 2
CAP = 4
HIGHEST = lax.Precision.HIGHEST


def padded_2(block, sides, width):
    for axis, dim in sides:
        count = lax.axis_size(axis)
        forward = [(i, i + 1) for i in range(count - 1)]
        backward = [(target, source) for source, target in forward]
        low = lax.ppermute(
            lax.slice_in_dim(block, block.shape[dim] - width, None, axis=dim), axis, forward
        )
        high = lax.ppermute(lax.slice_in_dim(block, 0, width, axis=dim), axis, backward)
        block = jnp.concatenate([low, block, high], axis=dim)
    return block


def neighbour_sum(conductances, padded):
    summed = conductances[0] * padded[2:, 1:-1, 1:-1] + conductances[1] * padded[:-2, 1:-1, 1:-1]
    summed = (
        summed
        + conductances[2] * padded[1:-1, 2:, 1:-1]
        + conductances[3] * padded[1:-1, :-2, 1:-1]
    )
    summed = (
        summed
        + conductances[4] * padded[1:-1, 1:-1, 2:]
        + conductances[5] * padded[1:-1, 1:-1, :-2]
    )
    return summed


def face_conductances(conductivity):
    padded = padded_2(conductivity, (("gx", 1), ("gy", 2), ("gz", 0)), 1)
    return (
        0.5 * (padded[2:, 1:-1, 1:-1] + conductivity),
        0.5 * (padded[:-2, 1:-1, 1:-1] + conductivity),
        0.5 * (padded[1:-1, 2:, 1:-1] + conductivity),
        0.5 * (padded[1:-1, :-2, 1:-1] + conductivity),
        0.5 * (padded[1:-1, 1:-1, 2:] + conductivity),
        0.5 * (padded[1:-1, 1:-1, :-2] + conductivity),
    )


def apply_global(field, conductances, diagonal):
    padded = padded_2(field.astype(jnp.bfloat16), (("gx", 1), ("gy", 2), ("gz", 0)), 1).astype(
        field.dtype
    )
    return diagonal * field - neighbour_sum(conductances, padded)


def local_solve(rhs, conductances, diagonal):
    iterate = jnp.zeros_like(rhs)
    remain = rhs
    scaled = remain / diagonal
    search = scaled
    inner_rz = jnp.sum(remain * scaled)
    for sweep_index in range(INNER):
        applied = diagonal * search - neighbour_sum(conductances, jnp.pad(search, 1))
        step_size = inner_rz / jnp.sum(search * applied)
        iterate = iterate + step_size * search
        remain = remain - step_size * applied
        scaled = remain / diagonal
        inner_next = jnp.sum(remain * scaled)
        search = scaled + inner_next / inner_rz * search
        inner_rz = inner_next
    return iterate


def dispatch_table(zone_of_block, zone_count):
    zone_vec = zone_of_block[:, 0]
    hits = (zone_vec[:, None] == jnp.arange(zone_count, dtype=jnp.int32)[None, :]).astype(jnp.int32)
    before = jnp.cumsum(hits, axis=0) - hits
    slot_of = jnp.sum(before * hits, axis=1)
    slot_hits = (slot_of[:, None] == jnp.arange(CAP, dtype=jnp.int32)[None, :]).astype(jnp.int32)
    dispatch = hits[:, :, None] * slot_hits[:, None, :]
    return dispatch.reshape(zone_vec.shape[0], zone_count * CAP).astype(jnp.bfloat16)


def lift_return(received, factor):
    lifted = jnp.einsum("sif,fg->sig", received, factor, preferred_element_type=jnp.float32).astype(
        jnp.bfloat16
    )
    return jnp.einsum("sig,fg->sif", lifted, factor, preferred_element_type=jnp.float32).astype(
        jnp.bfloat16
    )


def per_device(
    source_residual, storage, conductivity, primal_label, zone_of_block, coarse_factor, zone_factor
):
    conductances = face_conductances(conductivity)
    diagonal = (
        storage
        + conductances[0]
        + conductances[1]
        + conductances[2]
        + conductances[3]
        + conductances[4]
        + conductances[5]
    )
    onehot = (primal_label.reshape(-1)[:, None] == jnp.arange(KC, dtype=jnp.int32)[None, :]).astype(
        jnp.float32
    )
    zone_count = lax.axis_size(("gx", "gy", "gz"))
    dispatch = dispatch_table(zone_of_block, zone_count)
    factor = zone_factor[0]
    cells_z, cells_x, cells_y = source_residual.shape

    def refine_term(field):
        layers = jnp.concatenate([field[:2], field[-2:]], axis=0)
        blocks = layers.reshape(-1, FB).astype(jnp.bfloat16)
        outgoing = jnp.einsum(
            "bs,bf->sf", dispatch, blocks, preferred_element_type=jnp.float32
        ).astype(jnp.bfloat16)
        outgoing = outgoing.reshape(zone_count, CAP, FB)
        returned = lax.all_to_all(
            lift_return(
                lax.all_to_all(
                    outgoing, ("gx", "gy", "gz"), split_axis=0, concat_axis=0, tiled=True
                ),
                factor,
            ),
            ("gx", "gy", "gz"),
            split_axis=0,
            concat_axis=0,
            tiled=True,
        )
        returned = returned.reshape(zone_count * CAP, FB)
        placed = jnp.dot(dispatch, returned, preferred_element_type=jnp.float32)
        placed = placed.reshape(4, cells_x, cells_y)
        middle = jnp.zeros((cells_z - 4, cells_x, cells_y), jnp.float32)
        return jnp.concatenate([placed[:2], middle, placed[2:]], axis=0)

    def coarse_partial(field):
        line_values = jnp.sum(field, axis=2).reshape(-1)
        restricted = jnp.dot(line_values, onehot, precision=HIGHEST)
        return jnp.dot(restricted, coarse_factor, precision=HIGHEST)

    def coarse_vector(field):
        return lax.psum(coarse_partial(field), ("gx", "gy", "gz"))

    def product_sum(value):
        return lax.psum(value, ("gx", "gy", "gz"))

    def precondition(field, summed):
        coarse_coef = jnp.dot(coarse_factor, summed, precision=HIGHEST)
        line_values = jnp.dot(onehot, coarse_coef, precision=HIGHEST).reshape(cells_z, cells_x, 1)
        return local_solve(field, conductances, diagonal) + line_values + refine_term(field)

    solution = jnp.zeros_like(source_residual)
    residual = source_residual
    summed = coarse_vector(residual)
    precond = precondition(residual, summed)
    current_rz = product_sum(jnp.sum(residual * precond))
    direction = precond
    for outer_step in range(ITERS):
        applied = apply_global(direction, conductances, diagonal)
        final_step = outer_step + 1 == ITERS
        curvature = lax.psum(jnp.sum(direction * applied), ("gx", "gy", "gz"))
        step_size = current_rz / curvature
        solution = solution + step_size * direction
        residual = residual - step_size * applied
        if not final_step:
            summed = coarse_vector(residual)
            precond = precondition(residual, summed)
            next_rz = product_sum(jnp.sum(residual * precond))
            direction = precond + next_rz / current_rz * direction
            current_rz = next_rz
    return (solution, residual)


def solution(mesh):
    in_specs = (
        P("gz", "gx", "gy"),
        P("gz", "gx", "gy"),
        P("gz", "gx", "gy"),
        P("gz", "gx", "gy"),
        P(("gx", "gy", "gz"), None),
        P(("gx", "gy", "gz"), None),
        P(("gx", "gy", "gz"), None, None),
    )
    out_specs = (P("gz", "gx", "gy"), P("gz", "gx", "gy"))
    return jax.shard_map(
        per_device, mesh=mesh, in_specs=in_specs, out_specs=out_specs, check_vma=False
    )
```

profile of v0, /device:TPU:1, one launch (start us, length us, event | category | flops | bytes accessed | tf_op | source)
XLA Modules:
  0.0 639.4 jit_solution(13267346616168054444)
XLA Ops:
  1.7 3.3 collective-permute-start.1
  5.0 3.5 collective-permute-start
  11.7 3.1 collective-permute-start.2
  16.2 5.5 collective-permute-done.2
  21.8 4.1 collective-permute-done.3
  27.3 4.6 collective-permute-start.5
  33.5 2.4 fusion.261
  35.9 2.3 fusion.241
  39.0 66.3 %psum.42 = f32[4096]{0:T(1024)S(1)} all-reduce(f32[4096]{0:T(1024)S(1)} %bitcast.65), channel_id=1, replica_groups=mesh['gx'=8,'gy'=4,'gz'=4] {'gx','gy','gz'}, use_global_device_ids=true, to_apply=%region_17.18 | all-reduce | flops 4096 | bytes 32768 | tf_op jit(solution)/shard_map/psum | solution.py:150
  107.6 3.2 multiply_reduce_fusion.31
  115.5 6.6 %all-to-all-start = ((bf16[128,4,256]{2,1,0:T(4,128)(2,1)}), bf16[128,4,256]{2,1,0:T(4,128)(2,1)}, u32[]{:S(2)}, u32[]{:S(2)}) async-start(bf16[128,4,256]{2,1,0:T(4,128)(2,1)} %reshape.106), calls=%async_computation | async-start | bytes 524288 | tf_op jit(solution)/shard_map/all_to_all | solution.py:128
  123.5 2.2 multiply_reduce_fusion.30
  127.0 2.9 multiply_reduce_fusion.29
  132.6 2.2 multiply_reduce_fusion.28
  136.1 2.9 multiply_reduce_fusion.27
  141.7 2.2 multiply_reduce_fusion.26
  145.2 2.9 multiply_reduce_fusion.25
  150.7 2.2 multiply_reduce_fusion.24
  154.0 2.9 multiply_reduce_fusion.23
  159.5 2.2 multiply_reduce_fusion.22
  163.0 2.9 multiply_reduce_fusion.21
  168.6 2.2 multiply_reduce_fusion.20
  175.3 2.3 multiply_add_fusion.9
  177.6 2.2 convolution_convert_fusion.3
  181.7 10.2 %all-to-all-start.1 = ((bf16[128,4,256]{2,1,0:T(4,128)(2,1)}), bf16[128,4,256]{2,1,0:T(4,128)(2,1)}, u32[]{:S(2)}, u32[]{:S(2)}) async-start(bf16[128,4,256]{2,1,0:T(4,128)(2,1)} %copy.23), calls=%async_computation.1 | async-start | bytes 524288 | tf_op jit(solution)/shard_map/all_to_all | solution.py:126
  191.9 3.9 fusion.219
  197.1 5.6 all-to-all-done.1
  203.9 2.6 fusion.253
  206.6 3.1 collective-permute-start.6
  211.7 3.1 collective-permute-done.7
  215.1 2.2 collective-permute-start.8
  219.8 4.3 collective-permute-done.9
  224.2 2.3 collective-permute-start.10
  227.8 3.8 collective-permute-done.11
  232.0 2.4 multiply_reduce_fusion.17
  234.4 73.4 %all-reduce.16 = (f32[]{:T(128)}, f32[]{:T(128)}) all-reduce(f32[]{:T(128)} %get-tuple-element.6, f32[]{:T(128)} %get-tuple-element.5), channel_id=1, replica_groups=mesh['gx'=8,'gy'=4,'gz'=4] {'gx','gy','gz'}, use_global_device_ids=true, to_apply=%region_21.22 | all-reduce | flops 2 | bytes 16 | tf_op jit(solution)/shard_map/psum | solution.py:153
  310.6 2.3 fusion.240
  313.6 64.2 %psum.45 = f32[4096]{0:T(1024)S(1)} all-reduce(f32[4096]{0:T(1024)S(1)} %bitcast.67), channel_id=1, replica_groups=mesh['gx'=8,'gy'=4,'gz'=4] {'gx','gy','gz'}, use_global_device_ids=true, to_apply=%region_41.42 | all-reduce | flops 4096 | bytes 32768 | tf_op jit(solution)/shard_map/psum | solution.py:150
  379.9 3.1 multiply_reduce_fusion.14
  387.7 5.5 all-to-all-start.2
  394.6 2.2 multiply_reduce_fusion.13
  398.0 2.9 multiply_reduce_fusion.12
  403.4 2.1 multiply_reduce_fusion.11
  406.7 2.9 multiply_reduce_fusion.10
  412.2 2.1 multiply_reduce_fusion.9
  415.6 3.0 multiply_reduce_fusion.8
  421.2 2.2 multiply_reduce_fusion.7
  424.6 3.0 multiply_reduce_fusion.6
  430.2 2.2 multiply_reduce_fusion.5
  433.8 3.0 multiply_reduce_fusion.4
  439.5 2.2 multiply_reduce_fusion.3
  446.3 2.4 multiply_add_fusion.2
  452.6 10.4 %all-to-all-start.3 = ((bf16[128,4,256]{2,1,0:T(4,128)(2,1)}), bf16[128,4,256]{2,1,0:T(4,128)(2,1)}, u32[]{:S(2)}, u32[]{:S(2)}) async-start(bf16[128,4,256]{2,1,0:T(4,128)(2,1)} %copy.27), calls=%async_computation.3 | async-start | bytes 524288 | tf_op jit(solution)/shard_map/all_to_all | solution.py:126
  463.0 3.8 fusion.218
  468.1 5.7 all-to-all-done.3
  475.0 4.2 multiply_reduce_fusion.1
  479.2 62.7 %psum.46 = f32[]{:T(128)} all-reduce(f32[]{:T(128)} %get-tuple-element.16), channel_id=1, replica_groups=mesh['gx'=8,'gy'=4,'gz'=4] {'gx','gy','gz'}, use_global_device_ids=true, to_apply=%region_43.44 | all-reduce | flops 1 | bytes 8 | tf_op jit(solution)/shard_map/psum | solution.py:153
  544.5 3.3 collective-permute-start.12
  549.7 3.1 collective-permute-done.13
  557.3 4.2 collective-permute-done.15
  565.0 3.6 collective-permute-done.17
  569.1 2.2 multiply_reduce_fusion
  571.3 63.8 %psum.47 = f32[]{:T(128)} all-reduce(f32[]{:T(128)} %get-tuple-element.12), channel_id=1, replica_groups=mesh['gx'=8,'gy'=4,'gz'=4] {'gx','gy','gz'}, use_global_device_ids=true, to_apply=%region_45.46 | all-reduce | flops 1 | bytes 8 | tf_op jit(solution)/shard_map/psum | solution.py:169
  636.4 2.7 multiply_subtract_fusion
  (177 shorter events, 66.5 us)
Async XLA Ops:
  0.6 38.0 %copy-start = (f32[32,4096]{1,0:T(8,128)S(1)}, f32[32,4096]{1,0:T(8,128)}, u32[]{:S(2)}) copy-start(f32[32,4096]{1,0:T(8,128)} %param.12) | copy-start | bytes 1572868
  1.7 8.6 %collective-permute-start.1 = (f32[16,1,256]{2,1,0:T(1,128)S(1)}, f32[16,1,256]{2,1,0:T(1,128)S(1)}, u32[]{:S(2)}, u32[]{:S(2)}) collective-permute-start(f32[16,1,256]{2,1,0:T(1,128)S(1)} %get-tuple-element.101), channel_id=1, source_target_pairs={{16,0},{32,16},{48,32},{64,48},{80,64},{96,80},{112,96},{17,1},{33... | collective-permute-start | bytes 49160 | tf_op jit(solution)/shard_map/ppermute | solution.py:22
  5.0 5.3 collective-permute-start
  10.3 15.6 %copy-start.1 = (f32[16,32,256]{2,1,0:T(8,128)S(1)}, f32[16,32,256]{2,1,0:T(8,128)}, u32[]{:S(2)}) copy-start(f32[16,32,256]{2,1,0:T(8,128)} %param.9) | copy-start | bytes 1572868
  11.7 20.9 %copy-start.41 = (s32[16,32,1]{1,2,0:T(1,128)S(1)}, s32[16,32,1]{1,2,0:T(1,128)}, u32[]{:S(2)}) copy-start(s32[16,32,1]{1,2,0:T(1,128)} %param.10) | copy-start | bytes 6148
  11.7 10.1 %collective-permute-start.2 = (f32[16,34,1]{2,1,0:T(8,128)S(1)}, f32[16,34,1]{2,1,0:T(8,128)S(1)}, u32[]{:S(2)}, u32[]{:S(2)}) collective-permute-start(f32[16,34,1]{2,1,0:T(8,128)S(1)} %get-tuple-element.93), channel_id=1, source_target_pairs={{0,4},{4,8},{8,12},{1,5},{5,9},{9,13},{2,6},{6,10},{10,14},{3,7},{... | collective-permute-start | bytes 6536 | tf_op jit(solution)/shard_map/ppermute | solution.py:19
  14.8 11.0 %collective-permute-start.3 = (f32[16,34,1]{2,1,0:T(8,128)S(1)}, f32[16,34,1]{2,1,0:T(8,128)S(1)}, u32[]{:S(2)}, u32[]{:S(2)}) collective-permute-start(f32[16,34,1]{2,1,0:T(8,128)S(1)} %get-tuple-element.94), channel_id=1, source_target_pairs={{4,0},{8,4},{12,8},{5,1},{9,5},{13,9},{6,2},{10,6},{14,10},{7,3},{... | collective-permute-start | bytes 6536 | tf_op jit(solution)/shard_map/ppermute | solution.py:22
  21.8 11.7 %copy-start.39 = (f32[16,34,1]{2,1,0:T(8,128)}, f32[16,34,1]{2,1,0:T(8,128)S(1)}, u32[]{:S(2)}) copy-start(f32[16,34,1]{2,1,0:T(8,128)S(1)} %collective-permute-done.2) | copy-start | bytes 6532
  25.9 7.6 %copy-start.40 = (f32[16,34,1]{2,1,0:T(8,128)}, f32[16,34,1]{2,1,0:T(8,128)S(1)}, u32[]{:S(2)}) copy-start(f32[16,34,1]{2,1,0:T(8,128)S(1)} %collective-permute-done.3) | copy-start | bytes 6532
  26.0 7.5 %collective-permute-start.4 = (f32[1,34,258]{2,1,0:T(8,128)S(1)}, f32[1,34,258]{2,1,0:T(8,128)S(1)}, u32[]{:S(2)}, u32[]{:S(2)}) collective-permute-start(f32[1,34,258]{2,1,0:T(8,128)S(1)} %get-tuple-element.91), channel_id=1, source_target_pairs={{1,0},{2,1},{3,2},{5,4},{6,5},{7,6},{9,8},{10,9},{11,10},{13,12},{... | collective-permute-start | bytes 105272 | tf_op jit(solution)/shard_map/ppermute | solution.py:22
  27.3 6.2 collective-permute-start.5
  33.5 2.5 copy-start.20
  35.9 2.3 copy-start.2
  35.9 2.3 copy-start.37
  115.5 62.1 %all-to-all-start = ((bf16[128,4,256]{2,1,0:T(4,128)(2,1)}), bf16[128,4,256]{2,1,0:T(4,128)(2,1)}, u32[]{:S(2)}, u32[]{:S(2)}) async-start(bf16[128,4,256]{2,1,0:T(4,128)(2,1)} %reshape.106), calls=%async_computation | async-start | bytes 524288 | tf_op jit(solution)/shard_map/all_to_all | solution.py:128
  122.1 1.4 copy-start.3
  123.5 2.2 copy-start.26
  131.2 1.4 copy-start.4
  132.6 2.2 copy-start.28
  140.3 1.4 copy-start.5
  141.7 2.2 copy-start.30
  149.3 1.4 copy-start.6
  150.6 2.2 copy-start.32
  158.1 1.4 copy-start.7
  159.5 2.2 copy-start.34
  167.2 1.4 copy-start.8
  168.5 2.2 copy-start.23
  181.7 21.0 %all-to-all-start.1 = ((bf16[128,4,256]{2,1,0:T(4,128)(2,1)}), bf16[128,4,256]{2,1,0:T(4,128)(2,1)}, u32[]{:S(2)}, u32[]{:S(2)}) async-start(bf16[128,4,256]{2,1,0:T(4,128)(2,1)} %copy.23), calls=%async_computation.1 | async-start | bytes 524288 | tf_op jit(solution)/shard_map/all_to_all | solution.py:126
  202.7 1.2 copy-start.24
  206.6 25.4 %copy-start.35 = (f32[16,32,256]{2,1,0:T(8,128)}, f32[16,32,256]{2,1,0:T(8,128)S(1)}, u32[]{:S(2)}) copy-start(f32[16,32,256]{2,1,0:T(8,128)S(1)} %get-tuple-element.53) | copy-start | bytes 1572868
  206.6 5.1 collective-permute-start.6
  209.8 5.1 collective-permute-start.7
  215.1 4.7 collective-permute-start.8
  217.3 14.7 %copy-start.9 = (f32[16,32,256]{2,1,0:T(8,128)S(1)}, f32[16,32,256]{2,1,0:T(8,128)}, u32[]{:S(2)}) copy-start(f32[16,32,256]{2,1,0:T(8,128)} %copy-done.2) | copy-start | bytes 1572868
  217.3 14.7 %copy-start.21 = (f32[16,32,256]{2,1,0:T(8,128)S(1)}, f32[16,32,256]{2,1,0:T(8,128)}, u32[]{:S(2)}) copy-start(f32[16,32,256]{2,1,0:T(8,128)} %param.7) | copy-start | bytes 1572868
  217.3 6.7 %collective-permute-start.9 = (bf16[16,34,1]{2,1,0:T(8,128)(2,1)S(1)}, bf16[16,34,1]{2,1,0:T(8,128)(2,1)S(1)}, u32[]{:S(2)}, u32[]{:S(2)}) collective-permute-start(bf16[16,34,1]{2,1,0:T(8,128)(2,1)S(1)} %get-tuple-element.106), channel_id=1, source_target_pairs={{4,0},{8,4},{12,8},{5,1},{9,5},{13,9},{6,2},{10,6},{14,10},{7,3},{... | collective-permute-start | bytes 3272 | tf_op jit(solution)/shard_map/ppermute | solution.py:22
  224.2 3.6 collective-permute-start.10
  226.4 5.1 collective-permute-start.11
  309.1 1.4 copy-start.10
  310.5 2.3 copy-start.18
  310.6 2.3 copy-start.36
  387.7 61.0 %all-to-all-start.2 = ((bf16[128,4,256]{2,1,0:T(4,128)(2,1)}), bf16[128,4,256]{2,1,0:T(4,128)(2,1)}, u32[]{:S(2)}, u32[]{:S(2)}) async-start(bf16[128,4,256]{2,1,0:T(4,128)(2,1)} %reshape.108), calls=%async_computation.2 | async-start | bytes 524288 | tf_op jit(solution)/shard_map/all_to_all | solution.py:128
  393.2 1.4 copy-start.11
  394.6 2.2 copy-start.25
  402.0 1.4 copy-start.12
  403.4 2.1 copy-start.27
  410.8 1.4 copy-start.13
  412.2 2.2 copy-start.29
  419.8 1.4 copy-start.14
  421.2 2.2 copy-start.31
  428.9 1.4 copy-start.15
  430.2 2.2 copy-start.33
  438.1 1.4 copy-start.16
  439.5 2.2 copy-start.22
  446.3 2.4 copy-start.42
  452.6 21.2 %all-to-all-start.3 = ((bf16[128,4,256]{2,1,0:T(4,128)(2,1)}), bf16[128,4,256]{2,1,0:T(4,128)(2,1)}, u32[]{:S(2)}, u32[]{:S(2)}) async-start(bf16[128,4,256]{2,1,0:T(4,128)(2,1)} %copy.27), calls=%async_computation.3 | async-start | bytes 524288 | tf_op jit(solution)/shard_map/all_to_all | solution.py:126
  544.5 24.6 %copy-start.38 = (f32[16,32,256]{2,1,0:T(8,128)}, f32[16,32,256]{2,1,0:T(8,128)S(1)}, u32[]{:S(2)}) copy-start(f32[16,32,256]{2,1,0:T(8,128)S(1)} %get-tuple-element.15) | copy-start | bytes 1572868
  544.5 5.2 collective-permute-start.12
  547.8 5.1 collective-permute-start.13
  553.1 4.1 collective-permute-start.14
  554.5 14.6 %copy-start.17 = (f32[16,32,256]{2,1,0:T(8,128)S(1)}, f32[16,32,256]{2,1,0:T(8,128)}, u32[]{:S(2)}) copy-start(f32[16,32,256]{2,1,0:T(8,128)} %copy-done.2) | copy-start | bytes 1572868
  554.5 7.0 %collective-permute-start.15 = (bf16[16,34,1]{2,1,0:T(8,128)(2,1)S(1)}, bf16[16,34,1]{2,1,0:T(8,128)(2,1)S(1)}, u32[]{:S(2)}, u32[]{:S(2)}) collective-permute-start(bf16[16,34,1]{2,1,0:T(8,128)(2,1)S(1)} %get-tuple-element.104), channel_id=1, source_target_pairs={{4,0},{8,4},{12,8},{5,1},{9,5},{13,9},{6,2},{10,6},{14,10},{7,3},{... | collective-permute-start | bytes 3272 | tf_op jit(solution)/shard_map/ppermute | solution.py:22
  561.6 3.4 collective-permute-start.16
  563.5 5.1 collective-permute-start.17
  (1 other events, 1.2 us)
where the time goes:
time: 647 us; the launch traced here: 639 us
  blocking collectives  330 us (51%)
  other arithmetic  123 us (19%)
  starting transfers between devices  73.5 us (11%)
  waiting for transfers between devices  45.4 us (7%)
  between operations  43.5 us (7%)
  local copies, waits for them, and re-layouts  11.7 us (2%)
  matrix products  11.4 us (2%)
    psum x2, blocking collectives, product_sum(): return lax.psum(value, ('gx', 'gy', 'gz'))  136 us
    psum x2, blocking collectives, coarse_vector(): return lax.psum(coarse_partial(field), ('gx', 'gy', 'gz'))  131 us
    psum x1, blocking collectives, per_device(): curvature = lax.psum(jnp.sum(direction * applied), ('gx', 'gy', 'gz'))  63.8 us
    reduce_sum x14, other arithmetic, local_solve(): inner_next = jnp.sum(remain * scaled)  39.8 us
    reduce_sum x14, other arithmetic, local_solve(): step_size = inner_rz / jnp.sum(search * applied)  33.9 us
    ppermute x9, waiting for transfers between devices, padded_2(): lax.ppermute(lax.slice_in_dim(block, 0, width, axis=dim), axis, backward)  26.2 us
    ppermute x9, starting transfers between devices, padded_2(): lax.ppermute(lax.slice_in_dim(block, block.shape[dim] - width, None, axis...  25.4 us
    add x14, other arithmetic, local_solve(): search = scaled + inner_next / inner_rz * search  20.8 us
  transfers between devices with their start and end apart: 22, of which 12 were waited for; matrix products, arithmetic and copies ran while one was open for 14% of the time, Pallas kernels for 0%

commit v1 on v0

--- a/solution.py
+++ b/solution.py
@@ -150,7 +150,10 @@
         return lax.psum(coarse_partial(field), ("gx", "gy", "gz"))
 
     def product_sum(value):
-        return lax.psum(value, ("gx", "gy", "gz"))
+        prepare_loads = lambda local_values, shard_axis: jnp.sum(
+            lax.all_gather(local_values, shard_axis), 0
+        )
+        return prepare_loads(value, ("gx", "gy", "gz"))
 
     def precondition(field, summed):
         coarse_coef = jnp.dot(coarse_factor, summed, precision=HIGHEST)

time: 647 us -> 649 us (level)
  starting transfers between devices: 73.5 us -> 89.9 us
  waiting for transfers between devices: 45.4 us -> 31.9 us
    psum x2 -> x0, blocking collectives: 136 us -> none  [product_sum(): return lax.psum(value, ('gx', 'gy', 'gz'))]
    unnamed x0 -> x2, blocking collectives: none -> 127 us
    ppermute x9, starting transfers between devices: 25.4 us -> 46.2 us  [padded_2(): lax.ppermute(lax.slice_in_dim(block, block.shape[dim] - width, None, axis...]
    ppermute x9, waiting for transfers between devices: 26.2 us -> 14 us  [padded_2(): lax.ppermute(lax.slice_in_dim(block, 0, width, axis=dim), axis, backward)]
    all_to_all x2, starting transfers between devices: 20.6 us -> 10.5 us  [refine_term(): lax.all_to_all(lift_return(lax.all_to_all(outgoing, ('gx', 'gy', 'gz'), s...]
  transfers between devices with their start and end apart: 22 -> 22, of which waited for: 12 -> 13; matrix products, arithmetic and copies ran while one was open for 14% -> 15% of each run, Pallas kernels for 0% -> 0%
where the time goes in v1:
time: 649 us; the launch traced here: 642 us
  blocking collectives  326 us (50%)
  other arithmetic  128 us (20%)
  starting transfers between devices  89.9 us (14%)
  between operations  44.8 us (7%)
  waiting for transfers between devices  31.9 us (5%)
  local copies, waits for them, and re-layouts  10.9 us (2%)
  matrix products  10.7 us (2%)
    psum x2, blocking collectives, coarse_vector(): return lax.psum(coarse_partial(field), ('gx', 'gy', 'gz'))  135 us
    unnamed x2, blocking collectives  127 us
    psum x1, blocking collectives, per_device(): curvature = lax.psum(jnp.sum(direction * applied), ('gx', 'gy', 'gz'))  65 us
    ppermute x9, starting transfers between devices, padded_2(): lax.ppermute(lax.slice_in_dim(block, block.shape[dim] - width, None, axis...  46.2 us
    reduce_sum x14, other arithmetic, local_solve(): inner_next = jnp.sum(remain * scaled)  40 us
    reduce_sum x14, other arithmetic, local_solve(): step_size = inner_rz / jnp.sum(search * applied)  33.9 us
    add x14, other arithmetic, local_solve(): search = scaled + inner_next / inner_rz * search  20.8 us
    all_to_all x2, starting transfers between devices, refine_term(): lax.all_to_all(outgoing, ('gx', 'gy', 'gz'), split_axis=0, concat_axis=0,...  18.1 us
  transfers between devices with their start and end apart: 22, of which 13 were waited for; matrix products, arithmetic and copies ran while one was open for 15% of the time, Pallas kernels for 0%

profile of v1, /device:TPU:1, one launch (start us, length us, event | category | flops | bytes accessed | tf_op | source)
XLA Modules:
  0.0 642.2 jit_solution(2108157409736343637)
XLA Ops:
  1.7 4.9 collective-permute-start
  14.3 4.0 collective-permute-start.2
  18.4 4.4 collective-permute-done.3
  24.7 3.2 collective-permute-start.5
  30.9 2.8 collective-permute-done.4
  33.7 2.3 fusion.261
  36.1 2.3 fusion.241
  39.8 3.1 multiply_reduce_fusion.31
  45.6 13.0 %all-to-all-start = ((bf16[128,4,256]{2,1,0:T(4,128)(2,1)}), bf16[128,4,256]{2,1,0:T(4,128)(2,1)}, u32[]{:S(2)}, u32[]{:S(2)}) async-start(bf16[128,4,256]{2,1,0:T(4,128)(2,1)} %reshape.106), calls=%async_computation | async-start | bytes 524288 | tf_op jit(solution)/shard_map/all_to_all | solution.py:128
  59.4 67.7 %psum.28 = f32[4096]{0:T(1024)S(1)} all-reduce(f32[4096]{0:T(1024)S(1)} %bitcast.67), channel_id=1, replica_groups=mesh['gx'=8,'gy'=4,'gz'=4] {'gx','gy','gz'}, use_global_device_ids=true, to_apply=%region_17.18 | all-reduce | flops 4096 | bytes 32768 | tf_op jit(solution)/shard_map/psum | solution.py:150
  130.6 2.2 multiply_reduce_fusion.30
  134.2 3.0 multiply_reduce_fusion.29
  139.9 2.2 multiply_reduce_fusion.28
  143.4 2.9 multiply_reduce_fusion.27
  149.0 2.2 multiply_reduce_fusion.26
  152.5 3.0 multiply_reduce_fusion.25
  158.2 2.2 multiply_reduce_fusion.24
  161.7 2.9 multiply_reduce_fusion.23
  167.3 2.2 multiply_reduce_fusion.22
  170.9 2.9 multiply_reduce_fusion.21
  176.4 2.2 multiply_reduce_fusion.20
  183.1 2.4 multiply_add_fusion.9
  185.5 2.1 convolution_convert_fusion.3
  189.4 5.3 all-to-all-start.1
  194.7 3.9 fusion.219
  199.9 5.7 all-to-all-done.1
  206.9 3.4 fusion.253
  210.3 2.7 collective-permute-start.7
  213.0 2.9 collective-permute-start.6
  218.3 4.0 collective-permute-start.8
  222.3 2.8 collective-permute-done.9
  228.1 16.0 %collective-permute-start.10 = (bf16[1,34,258]{2,1,0:T(8,128)(2,1)}, bf16[1,34,258]{2,1,0:T(8,128)(2,1)S(1)}, u32[]{:S(2)}, u32[]{:S(2)}) collective-permute-start(bf16[1,34,258]{2,1,0:T(8,128)(2,1)} %get-tuple-element.97), channel_id=1, source_target_pairs={{0,1},{1,2},{2,3},{4,5},{5,6},{6,7},{8,9},{9,10},{10,11},{12,13},{... | collective-permute-start | bytes 52640 | tf_op jit(solution)/shard_map/ppermute | solution.py:19
  245.7 2.4 multiply_reduce_fusion.17
  248.9 63.9 %all-reduce.18 = (f32[128]{0:T(128)S(1)}, f32[]{:T(128)}) all-reduce(f32[128]{0:T(128)S(1)} %dynamic-update-slice, f32[]{:T(128)} %get-tuple-element.5), channel_id=1, replica_groups=mesh['gx'=8,'gy'=4,'gz'=4] {'gx','gy','gz'}, use_global_device_ids=true, to_apply=%add.16 | all-reduce | flops 129 | bytes 1032
  316.1 2.3 fusion.240
  319.7 3.2 multiply_reduce_fusion.14
  323.9 5.1 all-to-all-start.2
  329.8 67.3 %psum.30 = f32[4096]{0:T(1024)S(1)} all-reduce(f32[4096]{0:T(1024)S(1)} %bitcast.69), channel_id=1, replica_groups=mesh['gx'=8,'gy'=4,'gz'=4] {'gx','gy','gz'}, use_global_device_ids=true, to_apply=%region_41.42 | all-reduce | flops 4096 | bytes 32768 | tf_op jit(solution)/shard_map/psum | solution.py:150
  400.6 2.2 multiply_reduce_fusion.13
  404.1 3.0 multiply_reduce_fusion.12
  409.8 2.2 multiply_reduce_fusion.11
  413.2 3.0 multiply_reduce_fusion.10
  418.9 2.2 multiply_reduce_fusion.9
  422.4 3.0 multiply_reduce_fusion.8
  428.0 2.2 multiply_reduce_fusion.7
  431.5 3.0 multiply_reduce_fusion.6
  437.1 2.2 multiply_reduce_fusion.5
  440.6 3.0 multiply_reduce_fusion.4
  446.3 2.2 multiply_reduce_fusion.3
  453.0 2.4 multiply_add_fusion.2
  455.4 2.1 convolution_convert_fusion
  459.3 5.3 all-to-all-start.3
  464.6 3.8 fusion.218
  469.7 5.9 all-to-all-done.3
  476.8 4.3 multiply_reduce_fusion.1
  481.9 62.7 %all-reduce.17 = f32[128]{0:T(128)S(1)} all-reduce(f32[128]{0:T(128)S(1)} %dynamic-update-slice.1), channel_id=1, replica_groups=mesh['gx'=8,'gy'=4,'gz'=4] {'gx','gy','gz'}, use_global_device_ids=true, to_apply=%add.17 | all-reduce | flops 128 | bytes 1024
  547.9 2.7 collective-permute-start.13
  550.6 3.0 collective-permute-start.12
  555.9 4.1 collective-permute-start.14
  560.0 2.6 collective-permute-done.15
  565.1 4.0 collective-permute-start.16
  570.6 2.3 multiply_reduce_fusion
  572.9 65.0 %psum.31 = f32[]{:T(128)} all-reduce(f32[]{:T(128)} %get-tuple-element.12), channel_id=1, replica_groups=mesh['gx'=8,'gy'=4,'gz'=4] {'gx','gy','gz'}, use_global_device_ids=true, to_apply=%region_45.46 | all-reduce | flops 1 | bytes 8 | tf_op jit(solution)/shard_map/psum | solution.py:172
  639.2 2.7 multiply_subtract_fusion
  (195 shorter events, 65.4 us)
Async XLA Ops:
  0.6 58.4 %copy-start = (f32[32,4096]{1,0:T(8,128)S(1)}, f32[32,4096]{1,0:T(8,128)}, u32[]{:S(2)}) copy-start(f32[32,4096]{1,0:T(8,128)} %param.12) | copy-start | bytes 1572868
  1.7 8.6 %collective-permute-start = (f32[16,1,256]{2,1,0:T(1,128)S(1)}, f32[16,1,256]{2,1,0:T(1,128)S(1)}, u32[]{:S(2)}, u32[]{:S(2)}) collective-permute-start(f32[16,1,256]{2,1,0:T(1,128)S(1)} %get-tuple-element.102), channel_id=1, source_target_pairs={{0,16},{16,32},{32,48},{48,64},{64,80},{80,96},{96,112},{1,17},{17... | collective-permute-start | bytes 49160 | tf_op jit(solution)/shard_map/ppermute | solution.py:19
  6.6 5.1 collective-permute-start.1
  10.3 14.2 %copy-start.1 = (f32[16,32,256]{2,1,0:T(8,128)S(1)}, f32[16,32,256]{2,1,0:T(8,128)}, u32[]{:S(2)}) copy-start(f32[16,32,256]{2,1,0:T(8,128)} %param.9) | copy-start | bytes 1572868
  13.0 17.1 %copy-start.47 = (s32[16,32,1]{1,2,0:T(1,128)S(1)}, s32[16,32,1]{1,2,0:T(1,128)}, u32[]{:S(2)}) copy-start(s32[16,32,1]{1,2,0:T(1,128)} %param.10) | copy-start | bytes 6148
  13.0 9.8 %collective-permute-start.3 = (f32[16,34,1]{2,1,0:T(8,128)S(1)}, f32[16,34,1]{2,1,0:T(8,128)S(1)}, u32[]{:S(2)}, u32[]{:S(2)}) collective-permute-start(f32[16,34,1]{2,1,0:T(8,128)S(1)} %get-tuple-element.94), channel_id=1, source_target_pairs={{4,0},{8,4},{12,8},{5,1},{9,5},{13,9},{6,2},{10,6},{14,10},{7,3},{... | collective-permute-start | bytes 6536 | tf_op jit(solution)/shard_map/ppermute | solution.py:22
  14.3 10.3 %collective-permute-start.2 = (f32[16,34,1]{2,1,0:T(8,128)S(1)}, f32[16,34,1]{2,1,0:T(8,128)S(1)}, u32[]{:S(2)}, u32[]{:S(2)}) collective-permute-start(f32[16,34,1]{2,1,0:T(8,128)S(1)} %get-tuple-element.93), channel_id=1, source_target_pairs={{0,4},{4,8},{8,12},{1,5},{5,9},{9,13},{2,6},{6,10},{10,14},{3,7},{... | collective-permute-start | bytes 6536 | tf_op jit(solution)/shard_map/ppermute | solution.py:19
  22.8 8.1 %copy-start.41 = (f32[16,34,1]{2,1,0:T(8,128)}, f32[16,34,1]{2,1,0:T(8,128)S(1)}, u32[]{:S(2)}) copy-start(f32[16,34,1]{2,1,0:T(8,128)S(1)} %collective-permute-done.3) | copy-start | bytes 6532
  24.6 6.3 copy-start.42
  24.7 6.2 collective-permute-start.5
  27.9 5.8 collective-permute-start.4
  29.3 13.7 %copy-start.39 = (bf16[128,128,4]{0,2,1:T(4,128)(2,1)}, bf16[128,128,4]{0,2,1:T(4,128)(2,1)S(1)}, u32[]{:S(2)}) copy-start(bf16[128,128,4]{0,2,1:T(4,128)(2,1)S(1)} %multiply_convert_fusion) | copy-start | bytes 393220
  29.4 176.2 %copy-start.43 = (bf16[128,128,4]{1,0,2:T(8,128)(2,1)}, bf16[128,128,4]{1,0,2:T(8,128)(2,1)S(1)}, u32[]{:S(2)}) copy-start(bf16[128,128,4]{1,0,2:T(8,128)(2,1)S(1)} %copy.24) | copy-start | bytes 393220
  30.9 5.2 copy-start.20
  36.0 2.4 copy-start.2
  36.0 2.4 copy-start.37
  45.6 139.9 %all-to-all-start = ((bf16[128,4,256]{2,1,0:T(4,128)(2,1)}), bf16[128,4,256]{2,1,0:T(4,128)(2,1)}, u32[]{:S(2)}, u32[]{:S(2)}) async-start(bf16[128,4,256]{2,1,0:T(4,128)(2,1)} %reshape.106), calls=%async_computation | async-start | bytes 524288 | tf_op jit(solution)/shard_map/all_to_all | solution.py:128
  129.3 1.4 copy-start.3
  130.6 2.2 copy-start.26
  138.5 1.4 copy-start.4
  139.9 2.2 copy-start.28
  147.6 1.4 copy-start.5
  149.0 2.2 copy-start.30
  156.9 1.4 copy-start.6
  158.2 2.2 copy-start.32
  166.0 1.4 copy-start.7
  167.3 2.2 copy-start.34
  175.1 1.4 copy-start.8
  176.4 2.2 copy-start.23
  183.1 2.4 copy-start.48
  189.4 16.2 %all-to-all-start.1 = ((bf16[128,4,256]{2,1,0:T(4,128)(2,1)}), bf16[128,4,256]{2,1,0:T(4,128)(2,1)}, u32[]{:S(2)}, u32[]{:S(2)}) async-start(bf16[128,4,256]{2,1,0:T(4,128)(2,1)} %copy.23), calls=%async_computation.1 | async-start | bytes 524288 | tf_op jit(solution)/shard_map/all_to_all | solution.py:126
  210.3 5.6 collective-permute-start.7
  213.0 3.7 collective-permute-start.6
  217.0 8.1 %collective-permute-start.9 = (bf16[16,34,1]{2,1,0:T(8,128)(2,1)S(1)}, bf16[16,34,1]{2,1,0:T(8,128)(2,1)S(1)}, u32[]{:S(2)}, u32[]{:S(2)}) collective-permute-start(bf16[16,34,1]{2,1,0:T(8,128)(2,1)S(1)} %get-tuple-element.106), channel_id=1, source_target_pairs={{4,0},{8,4},{12,8},{5,1},{9,5},{13,9},{6,2},{10,6},{14,10},{7,3},{... | collective-permute-start | bytes 3272 | tf_op jit(solution)/shard_map/ppermute | solution.py:22
  218.3 7.7 %collective-permute-start.8 = (bf16[16,34,1]{2,1,0:T(8,128)(2,1)S(1)}, bf16[16,34,1]{2,1,0:T(8,128)(2,1)S(1)}, u32[]{:S(2)}, u32[]{:S(2)}) collective-permute-start(bf16[16,34,1]{2,1,0:T(8,128)(2,1)S(1)} %get-tuple-element.105), channel_id=1, source_target_pairs={{0,4},{4,8},{8,12},{1,5},{5,9},{9,13},{2,6},{6,10},{10,14},{3,7},{... | collective-permute-start | bytes 3272 | tf_op jit(solution)/shard_map/ppermute | solution.py:19
  226.8 17.3 %collective-permute-start.11 = (bf16[1,34,258]{2,1,0:T(8,128)(2,1)}, bf16[1,34,258]{2,1,0:T(8,128)(2,1)S(1)}, u32[]{:S(2)}, u32[]{:S(2)}) collective-permute-start(bf16[1,34,258]{2,1,0:T(8,128)(2,1)} %get-tuple-element.98), channel_id=1, source_target_pairs={{1,0},{2,1},{3,2},{5,4},{6,5},{7,6},{9,8},{10,9},{11,10},{13,12},{... | collective-permute-start | bytes 52640 | tf_op jit(solution)/shard_map/ppermute | solution.py:22
  228.1 16.1 %collective-permute-start.10 = (bf16[1,34,258]{2,1,0:T(8,128)(2,1)}, bf16[1,34,258]{2,1,0:T(8,128)(2,1)S(1)}, u32[]{:S(2)}, u32[]{:S(2)}) collective-permute-start(bf16[1,34,258]{2,1,0:T(8,128)(2,1)} %get-tuple-element.97), channel_id=1, source_target_pairs={{0,1},{1,2},{2,3},{4,5},{5,6},{6,7},{8,9},{9,10},{10,11},{12,13},{... | collective-permute-start | bytes 52640 | tf_op jit(solution)/shard_map/ppermute | solution.py:19
  244.1 1.6 copy-start.9
  244.1 1.6 copy-start.21
  244.1 1.6 copy-start.35
  314.7 1.4 copy-start.10
  316.1 2.3 copy-start.18
  316.1 2.3 copy-start.36
  319.6 3.3 copy-start.40
  323.9 131.5 %all-to-all-start.2 = ((bf16[128,4,256]{2,1,0:T(4,128)(2,1)}), bf16[128,4,256]{2,1,0:T(4,128)(2,1)S(1)}, u32[]{:S(2)}, u32[]{:S(2)}) async-start(bf16[128,4,256]{2,1,0:T(4,128)(2,1)} %reshape.108), calls=%async_computation.2 | async-start | bytes 524288 | tf_op jit(solution)/shard_map/all_to_all | solution.py:128
  399.3 1.4 copy-start.11
  400.6 2.2 copy-start.25
  408.4 1.4 copy-start.12
  409.8 2.2 copy-start.27
  418.9 2.2 copy-start.29
  428.0 2.2 copy-start.31
  435.7 1.4 copy-start.15
  437.1 2.2 copy-start.33
  446.3 2.2 copy-start.22
  459.3 16.2 %all-to-all-start.3 = ((bf16[128,4,256]{2,1,0:T(4,128)(2,1)}), bf16[128,4,256]{2,1,0:T(4,128)(2,1)}, u32[]{:S(2)}, u32[]{:S(2)}) async-start(bf16[128,4,256]{2,1,0:T(4,128)(2,1)} %copy.27), calls=%async_computation.3 | async-start | bytes 524288 | tf_op jit(solution)/shard_map/all_to_all | solution.py:126
  464.6 10.9 %copy-start.44 = (bf16[128,128,4]{1,0,2:T(8,128)(2,1)S(1)}, bf16[128,128,4]{1,0,2:T(8,128)(2,1)}, u32[]{:S(2)}) copy-start(bf16[128,128,4]{1,0,2:T(8,128)(2,1)} %copy-done.43) | copy-start | bytes 393220
  547.8 22.8 %copy-start.38 = (f32[16,32,256]{2,1,0:T(8,128)}, f32[16,32,256]{2,1,0:T(8,128)S(1)}, u32[]{:S(2)}) copy-start(f32[16,32,256]{2,1,0:T(8,128)S(1)} %get-tuple-element.15) | copy-start | bytes 1572868
  547.9 5.8 collective-permute-start.13
  550.6 3.7 collective-permute-start.12
  554.6 8.1 %collective-permute-start.15 = (bf16[16,34,1]{2,1,0:T(8,128)(2,1)S(1)}, bf16[16,34,1]{2,1,0:T(8,128)(2,1)S(1)}, u32[]{:S(2)}, u32[]{:S(2)}) collective-permute-start(bf16[16,34,1]{2,1,0:T(8,128)(2,1)S(1)} %get-tuple-element.104), channel_id=1, source_target_pairs={{4,0},{8,4},{12,8},{5,1},{9,5},{13,9},{6,2},{10,6},{14,10},{7,3},{... | collective-permute-start | bytes 3272 | tf_op jit(solution)/shard_map/ppermute | solution.py:22
  555.9 14.7 %copy-start.17 = (f32[16,32,256]{2,1,0:T(8,128)S(1)}, f32[16,32,256]{2,1,0:T(8,128)}, u32[]{:S(2)}) copy-start(f32[16,32,256]{2,1,0:T(8,128)} %copy-done.2) | copy-start | bytes 1572868
  555.9 7.9 %collective-permute-start.14 = (bf16[16,34,1]{2,1,0:T(8,128)(2,1)S(1)}, bf16[16,34,1]{2,1,0:T(8,128)(2,1)S(1)}, u32[]{:S(2)}, u32[]{:S(2)}) collective-permute-start(bf16[16,34,1]{2,1,0:T(8,128)(2,1)S(1)} %get-tuple-element.103), channel_id=1, source_target_pairs={{0,4},{4,8},{8,12},{1,5},{5,9},{9,13},{2,6},{6,10},{10,14},{3,7},{... | collective-permute-start | bytes 3272 | tf_op jit(solution)/shard_map/ppermute | solution.py:19
  563.8 5.3 collective-permute-start.17
  565.1 5.0 collective-permute-start.16
  (7 other events, 8.2 us)
